TPU v7x, 32 devices: a whole 2x2x4 slice. The times are simulated.
32 devices in a mesh: sample: 2 (over core), slab: 16 (over z, y, x).
Axes of the slice: x: 2, y: 2, z: 4, core: 2. Of those that a mesh axis runs over, the one named last changes fastest.
Arguments:
- force: float32 [3, 64, 32, 256], P(None, 'slab', None, 'sample'), parts along dimension 3, may hold values from -8 to 8, as said below
- modulus: float32 [64, 32, 256], P('slab', None, 'sample'), parts along dimension 2, may hold values from 0.2 to 1
Outputs:
- fine_field: float32 [3, 64, 32, 256], P(None, 'slab', None, 'sample'), parts along dimension 3
- coarse_field: float32 [3, 32, 16, 128], P(None, 'slab', None, 'sample'), parts along dimension 3
- compliance: float32 [4], P('sample'), parts along dimension 0
There are 2 independent parts, one for each index of `sample`. A program takes and returns all parts, laid end to end along the dimension named above; each array names one. Nothing has to cross between parts.
Inputs may be any that keep to these rules, and one draw needn't show every extreme that they name: Body force on each cell and component.
All inputs are finite; a program needn't handle non-finite values.
Results may differ from a plain program's by a relative error of at most 0.0001.
Values sent between devices are 32-bit elements; how exact they have to be, the bound alone decides.
A program may use at most 128 MiB of HBM per device.

v0:
```python
import jax
import jax.numpy as jnp
from jax import lax
from jax.sharding import PartitionSpec as P

ITERS = 2
SMOOTH = 2
CDEG = 4


def extended(block, sides, width):
    for axis, dim in sides:
        count = lax.axis_size(axis)
        forward = [(i, i + 1) for i in range(count - 1)]
        backward = [(target, source) for source, target in forward]
        low = lax.ppermute(
            lax.slice_in_dim(block, block.shape[dim] - width, None, axis=dim), axis, forward
        )
        high = lax.ppermute(lax.slice_in_dim(block, 0, width, axis=dim), axis, backward)
        block = jnp.concatenate([low, block, high], axis=dim)
    return block


def from_behind(x, axis, by):
    peers = lax.axis_size(axis)
    pairs = [(i, i + by) for i in range(peers) if 0 <= i + by < peers]
    return lax.ppermute(x, axis, pairs)


def shift_back(values, dimension):
    length = values.shape[dimension]
    zeroes = jnp.zeros_like(lax.slice_in_dim(values, 0, 1, axis=dimension))
    return jnp.concatenate(
        [zeroes, lax.slice_in_dim(values, 0, length - 1, axis=dimension)], axis=dimension
    )


def shift_ahead(values, dimension):
    length = values.shape[dimension]
    zeroes = jnp.zeros_like(lax.slice_in_dim(values, 0, 1, axis=dimension))
    return jnp.concatenate(
        [lax.slice_in_dim(values, 1, length, axis=dimension), zeroes], axis=dimension
    )


def operate_extended(padded, lame_ext):
    lower = padded[:, :-1]
    grad_z = padded[:, 1:] - lower
    grad_y = shift_ahead(lower, 2) - lower
    grad_x = shift_ahead(lower, 3) - lower
    spread = lame_ext * (grad_x[0] + grad_y[1] + grad_z[2])
    flux_z = lame_ext * grad_z
    inner_y = lame_ext[1:] * grad_y[:, 1:]
    inner_x = lame_ext[1:] * grad_x[:, 1:]
    inner_s = spread[1:]
    result = (
        flux_z[:, :-1]
        - flux_z[:, 1:]
        + (shift_back(inner_y, 2) - inner_y)
        + (shift_back(inner_x, 3) - inner_x)
    )
    pressure = jnp.stack(
        [shift_back(inner_s, 2) - inner_s, shift_back(inner_s, 1) - inner_s, spread[:-1] - inner_s]
    )
    return result + pressure


def operate_split(displace, lame_ext):
    padded = extended(displace, (("slab", 1),), 1)
    return operate_extended(padded, lame_ext)


def extend(lame):
    below = from_behind(lame[-1:], "slab", 1)
    return jnp.concatenate([below, lame], 0)


def diag_inverse(lame_ext):
    lame = lame_ext[1:]
    laplace = lame + lame_ext[:-1] + (lame + shift_back(lame, 1)) + (lame + shift_back(lame, 2))
    diagonal = jnp.stack(
        [
            laplace + lame + shift_back(lame, 2),
            laplace + lame + shift_back(lame, 1),
            laplace + lame + lame_ext[:-1],
        ]
    )
    return 1.0 / diagonal


def restrict_scalar(values):
    shape = values.shape
    return values.reshape(shape[0] // 2, 2, shape[1] // 2, 2, shape[2] // 2, 2).mean(axis=(1, 3, 5))


def restrict_vector(values):
    shape = values.shape
    return values.reshape(shape[0], shape[1] // 2, 2, shape[2] // 2, 2, shape[3] // 2, 2).mean(
        axis=(2, 4, 6)
    )


def prolong(values):
    return jnp.repeat(jnp.repeat(jnp.repeat(values, 2, 1), 2, 2), 2, 3)


def chebyshev(iterate, residue, operator, inverse, degree, low_end, high_end):
    centre = (high_end + low_end) / 2.0
    half_width = (high_end - low_end) / 2.0
    spread_ratio = centre / half_width
    rho_now = 1.0 / spread_ratio
    update = inverse * residue / centre
    for section in range(degree):
        iterate = iterate + update
        residue = residue - operator(update)
        if section + 1 < degree:
            rho_next = 1.0 / (2.0 * spread_ratio - rho_now)
            update = rho_next * rho_now * update + 2.0 * rho_next / half_width * (inverse * residue)
            rho_now = rho_next
    return (iterate, residue)


def body(force, modulus):
    lame = 0.4 * modulus
    lame_ext = extend(lame)
    fine_inverse = diag_inverse(lame_ext)

    def fine_operator(vector):
        return operate_split(vector, lame_ext)

    coarse_lame = restrict_scalar(lame)
    coarse_ext = extend(coarse_lame)
    coarse_inverse = diag_inverse(coarse_ext)

    def coarse_solve(rhs_local, degree):
        solved, unused = chebyshev(
            jnp.zeros_like(rhs_local),
            rhs_local,
            lambda vector: operate_split(vector, coarse_ext),
            coarse_inverse,
            degree,
            0.02,
            2.0,
        )
        return solved

    iterate = jnp.zeros_like(force)
    residue = force
    for cycle in range(ITERS):
        iterate, residue = chebyshev(
            iterate, residue, fine_operator, fine_inverse, SMOOTH, 0.25, 2.0
        )
        correction = coarse_solve(4.0 * restrict_vector(residue), CDEG)
        expanded = prolong(correction)
        iterate = iterate + expanded
        residue = residue - fine_operator(expanded)
        iterate, residue = chebyshev(
            iterate, residue, fine_operator, fine_inverse, SMOOTH, 0.25, 2.0
        )
    coarse_force = restrict_vector(force)
    coarse_field = coarse_solve(4.0 * coarse_force, 2 * CDEG)
    totals = lax.psum((jnp.sum(force * iterate), jnp.sum(coarse_force * coarse_field)), "slab")
    cells = float(lame.size * lax.axis_size("slab"))
    compliance = jnp.stack([totals[0] / cells, totals[1] / (cells / 8.0)])
    return (iterate, coarse_field, compliance)


def solution(mesh):
    return jax.shard_map(
        body,
        mesh=mesh,
        in_specs=(P(None, "slab", None, "sample"), P("slab", None, "sample")),
        out_specs=(P(None, "slab", None, "sample"), P(None, "slab", None, "sample"), P("sample")),
        check_vma=False,
    )
```

profile of v0, /device:TPU:0, one launch (start us, length us, event | category | flops | bytes accessed | tf_op | source)
XLA Modules:
  0.0 398.9 jit_solution(14483510734111546389)
XLA Ops:
  1.5 5.6 %reshape.86 = f32[2,2,16,2,64,2]{5,4,3,2,1,0:T(8,128)} reshape(f32[4,32,128]{2,1,0:T(8,128)S(1)} %broadcast_multiply_fusion.26) | data formatting | bytes 131072 | tf_op jit(solution)/shard_map/reshape | solution.py:93
  9.6 4.9 %collective-permute-start.3 = (f32[1,16,64]{2,1,0:T(8,128)S(1)}, f32[1,16,64]{2,1,0:T(8,128)S(1)}, u32[]{:S(2)}, u32[]{:S(2)}) collective-permute-start(f32[1,16,64]{2,1,0:T(8,128)S(1)} %slice.1690), channel_id=1, source_target_pairs={{0,1},{1,2},{2,3},{3,4},{4,5},{5,6},{6,7},{7,8},{8,9},{9,10},{10,1... | collective-permute-start | bytes 12296 | tf_op jit(solution)/shard_map/ppermute | solution.py:27
  19.3 14.6 %reshape.95 = f32[3,2,2,16,2,64,2]{6,5,4,3,2,1,0:T(8,128)} reshape(f32[3,4,32,128]{3,2,1,0:T(8,128)} %param.2) | data formatting | bytes 393216 | tf_op jit(solution)/shard_map/reshape | solution.py:98
  33.9 5.5 %reduce_sum.57 = f32[3,2,16,64]{3,2,1,0:T(8,128)S(1)} reduce(f32[3,2,2,16,2,64,2]{6,5,4,3,2,1,0:T(8,128)} %reshape.95, f32[]{:T(128)} %constant.27.clone.1), dimensions={2,4,6}, to_apply=%region_3.0 | reduce | flops 43008 | bytes 221188 | tf_op jit(solution)/shard_map/reduce_sum | solution.py:98
  40.8 4.5 %collective-permute-start.33 = (f32[3,1,16,64]{3,2,1,0:T(8,128)S(1)}, f32[3,1,16,64]{3,2,1,0:T(8,128)S(1)}, u32[]{:S(2)}, u32[]{:S(2)}) collective-permute-start(f32[3,1,16,64]{3,2,1,0:T(8,128)S(1)} %get-tuple-element.247), channel_id=1, source_target_pairs={{0,1},{1,2},{2,3},{3,4},{4,5},{5,6},{6,7},{7,8},{8,9},{9,10},{10,1... | collective-permute-start | bytes 36872 | tf_op jit(solution)/shard_map/ppermute | solution.py:16
  49.0 4.9 %collective-permute-start.35 = (f32[3,1,16,64]{3,2,1,0:T(8,128)S(1)}, f32[3,1,16,64]{3,2,1,0:T(8,128)S(1)}, u32[]{:S(2)}, u32[]{:S(2)}) collective-permute-start(f32[3,1,16,64]{3,2,1,0:T(8,128)S(1)} %get-tuple-element.245), channel_id=1, source_target_pairs={{0,1},{1,2},{2,3},{3,4},{4,5},{5,6},{6,7},{7,8},{8,9},{9,10},{10,1... | collective-permute-start | bytes 36872 | tf_op jit(solution)/shard_map/ppermute | solution.py:16
  55.9 5.1 %collective-permute-start.37 = (f32[3,1,16,64]{3,2,1,0:T(8,128)S(1)}, f32[3,1,16,64]{3,2,1,0:T(8,128)S(1)}, u32[]{:S(2)}, u32[]{:S(2)}) collective-permute-start(f32[3,1,16,64]{3,2,1,0:T(8,128)S(1)} %get-tuple-element.243), channel_id=1, source_target_pairs={{0,1},{1,2},{2,3},{3,4},{4,5},{5,6},{6,7},{7,8},{8,9},{9,10},{10,1... | collective-permute-start | bytes 36872 | tf_op jit(solution)/shard_map/ppermute | solution.py:16
  63.2 5.5 %collective-permute-done.36 = f32[3,1,16,64]{3,2,1,0:T(8,128)S(1)} collective-permute-done((f32[3,1,16,64]{3,2,1,0:T(8,128)S(1)}, f32[3,1,16,64]{3,2,1,0:T(8,128)S(1)}, u32[]{:S(2)}, u32[]{:S(2)}) %collective-permute-start.36) | collective-permute-done | bytes 12320 | tf_op jit(solution)/shard_map/ppermute | solution.py:19
  68.9 4.8 %collective-permute-start.39 = (f32[3,1,16,64]{3,2,1,0:T(8,128)S(1)}, f32[3,1,16,64]{3,2,1,0:T(8,128)S(1)}, u32[]{:S(2)}, u32[]{:S(2)}) collective-permute-start(f32[3,1,16,64]{3,2,1,0:T(8,128)S(1)} %get-tuple-element.241), channel_id=1, source_target_pairs={{0,1},{1,2},{2,3},{3,4},{4,5},{5,6},{6,7},{7,8},{8,9},{9,10},{10,1... | collective-permute-start | bytes 36872 | tf_op jit(solution)/shard_map/ppermute | solution.py:16
  75.2 5.3 %collective-permute-start.2 = (f32[3,1,32,128]{2,3,1,0:T(8,128)}, f32[3,1,32,128]{2,3,1,0:T(8,128)S(1)}, u32[]{:S(2)}, u32[]{:S(2)}) collective-permute-start(f32[3,1,32,128]{2,3,1,0:T(8,128)} %get-tuple-element.142), channel_id=1, source_target_pairs={{0,1},{1,2},{2,3},{3,4},{4,5},{5,6},{6,7},{7,8},{8,9},{9,10},{10,1... | collective-permute-start | bytes 147464 | tf_op jit(solution)/shard_map/ppermute | solution.py:16
  82.0 6.5 %collective-permute-done.38 = f32[3,1,16,64]{3,2,1,0:T(8,128)S(1)} collective-permute-done((f32[3,1,16,64]{3,2,1,0:T(8,128)S(1)}, f32[3,1,16,64]{3,2,1,0:T(8,128)S(1)}, u32[]{:S(2)}, u32[]{:S(2)}) %collective-permute-start.38) | collective-permute-done | bytes 12320 | tf_op jit(solution)/shard_map/ppermute | solution.py:19
  90.6 5.1 %collective-permute-start.41 = (f32[3,1,16,64]{3,2,1,0:T(8,128)S(1)}, f32[3,1,16,64]{3,2,1,0:T(8,128)S(1)}, u32[]{:S(2)}, u32[]{:S(2)}) collective-permute-start(f32[3,1,16,64]{3,2,1,0:T(8,128)S(1)} %get-tuple-element.239), channel_id=1, source_target_pairs={{0,1},{1,2},{2,3},{3,4},{4,5},{5,6},{6,7},{7,8},{8,9},{9,10},{10,1... | collective-permute-start | bytes 36872 | tf_op jit(solution)/shard_map/ppermute | solution.py:16
  101.1 5.7 %collective-permute-start.5 = (f32[3,1,32,128]{2,3,1,0:T(8,128)S(1)}, f32[3,1,32,128]{2,3,1,0:T(8,128)S(1)}, u32[]{:S(2)}, u32[]{:S(2)}) collective-permute-start(f32[3,1,32,128]{2,3,1,0:T(8,128)S(1)} %get-tuple-element.140), channel_id=1, source_target_pairs={{0,1},{1,2},{2,3},{3,4},{4,5},{5,6},{6,7},{7,8},{8,9},{9,10},{10,1... | collective-permute-start | bytes 147464 | tf_op jit(solution)/shard_map/ppermute | solution.py:16
  112.2 13.9 %reshape.87 = f32[3,2,2,16,2,64,2]{6,5,4,3,2,1,0:T(8,128)} reshape(f32[3,4,32,128]{3,2,1,0:T(8,128)S(1)} %copy.178) | data formatting | bytes 393216 | tf_op jit(solution)/shard_map/reshape | solution.py:98
  126.1 5.5 %reduce_sum.55 = f32[3,2,16,64]{3,2,1,0:T(8,128)S(1)} reduce(f32[3,2,2,16,2,64,2]{6,5,4,3,2,1,0:T(8,128)} %reshape.87, f32[]{:T(128)} %constant.27.clone.1), dimensions={2,4,6}, to_apply=%region_1.0 | reduce | flops 43008 | bytes 221188 | tf_op jit(solution)/shard_map/reduce_sum | solution.py:98
  133.2 5.3 %collective-permute-start.7 = (f32[3,1,16,64]{3,2,1,0:T(8,128)S(1)}, f32[3,1,16,64]{3,2,1,0:T(8,128)S(1)}, u32[]{:S(2)}, u32[]{:S(2)}) collective-permute-start(f32[3,1,16,64]{3,2,1,0:T(8,128)S(1)} %get-tuple-element.259), channel_id=1, source_target_pairs={{0,1},{1,2},{2,3},{3,4},{4,5},{5,6},{6,7},{7,8},{8,9},{9,10},{10,1... | collective-permute-start | bytes 36872 | tf_op jit(solution)/shard_map/ppermute | solution.py:16
  139.8 5.9 %collective-permute-start.43 = (f32[3,1,16,64]{3,2,1,0:T(8,128)S(1)}, f32[3,1,16,64]{3,2,1,0:T(8,128)S(1)}, u32[]{:S(2)}, u32[]{:S(2)}) collective-permute-start(f32[3,1,16,64]{3,2,1,0:T(8,128)S(1)} %get-tuple-element.236), channel_id=1, source_target_pairs={{0,1},{1,2},{2,3},{3,4},{4,5},{5,6},{6,7},{7,8},{8,9},{9,10},{10,1... | collective-permute-start | bytes 36872 | tf_op jit(solution)/shard_map/ppermute | solution.py:16
  147.2 5.3 %collective-permute-done.6 = f32[3,1,16,64]{3,2,1,0:T(8,128)S(1)} collective-permute-done((f32[3,1,16,64]{3,2,1,0:T(8,128)S(1)}, f32[3,1,16,64]{3,2,1,0:T(8,128)S(1)}, u32[]{:S(2)}, u32[]{:S(2)}) %collective-permute-start.6) | collective-permute-done | bytes 12320 | tf_op jit(solution)/shard_map/ppermute | solution.py:19
  154.1 6.2 %collective-permute-start.9 = (f32[3,1,16,64]{3,2,1,0:T(8,128)S(1)}, f32[3,1,16,64]{3,2,1,0:T(8,128)S(1)}, u32[]{:S(2)}, u32[]{:S(2)}) collective-permute-start(f32[3,1,16,64]{3,2,1,0:T(8,128)S(1)} %get-tuple-element.257), channel_id=1, source_target_pairs={{0,1},{1,2},{2,3},{3,4},{4,5},{5,6},{6,7},{7,8},{8,9},{9,10},{10,1... | collective-permute-start | bytes 36872 | tf_op jit(solution)/shard_map/ppermute | solution.py:16
  161.9 5.9 %collective-permute-done.8 = f32[3,1,16,64]{3,2,1,0:T(8,128)S(1)} collective-permute-done((f32[3,1,16,64]{3,2,1,0:T(8,128)S(1)}, f32[3,1,16,64]{3,2,1,0:T(8,128)S(1)}, u32[]{:S(2)}, u32[]{:S(2)}) %collective-permute-start.8) | collective-permute-done | bytes 12320 | tf_op jit(solution)/shard_map/ppermute | solution.py:19
  168.1 5.7 %collective-permute-start.11 = (f32[3,1,16,64]{3,2,1,0:T(8,128)S(1)}, f32[3,1,16,64]{3,2,1,0:T(8,128)S(1)}, u32[]{:S(2)}, u32[]{:S(2)}) collective-permute-start(f32[3,1,16,64]{3,2,1,0:T(8,128)S(1)} %get-tuple-element.255), channel_id=1, source_target_pairs={{0,1},{1,2},{2,3},{3,4},{4,5},{5,6},{6,7},{7,8},{8,9},{9,10},{10,1... | collective-permute-start | bytes 36872 | tf_op jit(solution)/shard_map/ppermute | solution.py:16
  183.0 4.8 %collective-permute-start.13 = (f32[3,1,32,128]{2,3,1,0:T(8,128)S(1)}, f32[3,1,32,128]{2,3,1,0:T(8,128)S(1)}, u32[]{:S(2)}, u32[]{:S(2)}) collective-permute-start(f32[3,1,32,128]{2,3,1,0:T(8,128)S(1)} %get-tuple-element.138), channel_id=1, source_target_pairs={{0,1},{1,2},{2,3},{3,4},{4,5},{5,6},{6,7},{7,8},{8,9},{9,10},{10,1... | collective-permute-start | bytes 147464 | tf_op jit(solution)/shard_map/ppermute | solution.py:16
  192.4 5.3 %collective-permute-done.12 = f32[3,1,32,128]{2,3,1,0:T(8,128)S(1)} collective-permute-done((f32[3,1,32,128]{2,3,1,0:T(8,128)S(1)}, f32[3,1,32,128]{2,3,1,0:T(8,128)S(1)}, u32[]{:S(2)}, u32[]{:S(2)}) %collective-permute-start.12) | collective-permute-done | bytes 49184 | tf_op jit(solution)/shard_map/ppermute | solution.py:19
  241.4 4.6 %collective-permute-start.21 = (f32[3,1,32,128]{2,3,1,0:T(8,128)S(1)}, f32[3,1,32,128]{2,3,1,0:T(8,128)S(1)}, u32[]{:S(2)}, u32[]{:S(2)}) collective-permute-start(f32[3,1,32,128]{2,3,1,0:T(8,128)S(1)} %get-tuple-element.130), channel_id=1, source_target_pairs={{0,1},{1,2},{2,3},{3,4},{4,5},{5,6},{6,7},{7,8},{8,9},{9,10},{10,1... | collective-permute-start | bytes 147464 | tf_op jit(solution)/shard_map/ppermute | solution.py:16
  257.6 13.9 %reshape.91 = f32[3,2,2,16,2,64,2]{6,5,4,3,2,1,0:T(8,128)} reshape(f32[3,4,32,128]{3,2,1,0:T(8,128)S(1)} %copy.185) | data formatting | bytes 393216 | tf_op jit(solution)/shard_map/reshape | solution.py:98
  271.5 5.5 %reduce_sum.56 = f32[3,2,16,64]{3,2,1,0:T(8,128)S(1)} reduce(f32[3,2,2,16,2,64,2]{6,5,4,3,2,1,0:T(8,128)} %reshape.91, f32[]{:T(128)} %constant.27.clone.1), dimensions={2,4,6}, to_apply=%region_2.0 | reduce | flops 43008 | bytes 221188 | tf_op jit(solution)/shard_map/reduce_sum | solution.py:98
  278.6 5.6 %collective-permute-start.23 = (f32[3,1,16,64]{3,2,1,0:T(8,128)S(1)}, f32[3,1,16,64]{3,2,1,0:T(8,128)S(1)}, u32[]{:S(2)}, u32[]{:S(2)}) collective-permute-start(f32[3,1,16,64]{3,2,1,0:T(8,128)S(1)} %get-tuple-element.253), channel_id=1, source_target_pairs={{0,1},{1,2},{2,3},{3,4},{4,5},{5,6},{6,7},{7,8},{8,9},{9,10},{10,1... | collective-permute-start | bytes 36872 | tf_op jit(solution)/shard_map/ppermute | solution.py:16
  291.7 4.9 %collective-permute-done.22 = f32[3,1,16,64]{3,2,1,0:T(8,128)S(1)} collective-permute-done((f32[3,1,16,64]{3,2,1,0:T(8,128)S(1)}, f32[3,1,16,64]{3,2,1,0:T(8,128)S(1)}, u32[]{:S(2)}, u32[]{:S(2)}) %collective-permute-start.22) | collective-permute-done | bytes 12320 | tf_op jit(solution)/shard_map/ppermute | solution.py:19
  298.3 4.8 %collective-permute-start.25 = (f32[3,1,16,64]{3,2,1,0:T(8,128)S(1)}, f32[3,1,16,64]{3,2,1,0:T(8,128)S(1)}, u32[]{:S(2)}, u32[]{:S(2)}) collective-permute-start(f32[3,1,16,64]{3,2,1,0:T(8,128)S(1)} %get-tuple-element.251), channel_id=1, source_target_pairs={{0,1},{1,2},{2,3},{3,4},{4,5},{5,6},{6,7},{7,8},{8,9},{9,10},{10,1... | collective-permute-start | bytes 36872 | tf_op jit(solution)/shard_map/ppermute | solution.py:16
  322.4 4.8 %collective-permute-start.29 = (f32[3,1,32,128]{2,3,1,0:T(8,128)S(1)}, f32[3,1,32,128]{2,3,1,0:T(8,128)S(1)}, u32[]{:S(2)}, u32[]{:S(2)}) collective-permute-start(f32[3,1,32,128]{2,3,1,0:T(8,128)S(1)} %get-tuple-element.128), channel_id=1, source_target_pairs={{0,1},{1,2},{2,3},{3,4},{4,5},{5,6},{6,7},{7,8},{8,9},{9,10},{10,1... | collective-permute-start | bytes 147464 | tf_op jit(solution)/shard_map/ppermute | solution.py:16
  345.2 5.3 %collective-permute-done.30 = f32[3,1,32,128]{2,3,1,0:T(8,128)S(1)} collective-permute-done((f32[3,1,32,128]{2,3,1,0:T(8,128)S(1)}, f32[3,1,32,128]{2,3,1,0:T(8,128)S(1)}, u32[]{:S(2)}, u32[]{:S(2)}) %collective-permute-start.30) | collective-permute-done | bytes 49184 | tf_op jit(solution)/shard_map/ppermute | solution.py:19
  356.5 40.5 %all-reduce.136 = (f32[]{:T(128)}, f32[]{:T(128)}) all-reduce(f32[]{:T(128)} %get-tuple-element.19, f32[]{:T(128)} %get-tuple-element.17), channel_id=1, replica_groups=mesh['sample'=2,'slab'=16] {'slab'}, use_global_device_ids=true, to_apply=%region_7.0 | all-reduce | flops 2 | bytes 16 | tf_op jit(solution)/shard_map/psum | solution.py:162
  (367 shorter events, 162.9 us)
Async XLA Ops:
  9.6 29.8 %collective-permute-start.3 = (f32[1,16,64]{2,1,0:T(8,128)S(1)}, f32[1,16,64]{2,1,0:T(8,128)S(1)}, u32[]{:S(2)}, u32[]{:S(2)}) collective-permute-start(f32[1,16,64]{2,1,0:T(8,128)S(1)} %slice.1690), channel_id=1, source_target_pairs={{0,1},{1,2},{2,3},{3,4},{4,5},{5,6},{6,7},{7,8},{8,9},{9,10},{10,1... | collective-permute-start | bytes 12296 | tf_op jit(solution)/shard_map/ppermute | solution.py:27
  14.5 32.6 %collective-permute-start = (f32[1,32,128]{2,1,0:T(8,128)S(1)}, f32[1,32,128]{2,1,0:T(8,128)S(1)}, u32[]{:S(2)}, u32[]{:S(2)}) collective-permute-start(f32[1,32,128]{2,1,0:T(8,128)S(1)} %slice.1666), channel_id=1, source_target_pairs={{0,1},{1,2},{2,3},{3,4},{4,5},{5,6},{6,7},{7,8},{8,9},{9,10},{10,1... | collective-permute-start | bytes 49160 | tf_op jit(solution)/shard_map/ppermute | solution.py:27
  39.5 7.5 %collective-permute-start.32 = (f32[3,1,16,64]{3,2,1,0:T(8,128)S(1)}, f32[3,1,16,64]{3,2,1,0:T(8,128)S(1)}, u32[]{:S(2)}, u32[]{:S(2)}) collective-permute-start(f32[3,1,16,64]{3,2,1,0:T(8,128)S(1)} %get-tuple-element.246), channel_id=1, source_target_pairs={{1,0},{2,1},{3,2},{4,3},{5,4},{6,5},{7,6},{8,7},{9,8},{10,9},{11,1... | collective-permute-start | bytes 36872 | tf_op jit(solution)/shard_map/ppermute | solution.py:19
  47.7 7.8 %collective-permute-start.34 = (f32[3,1,16,64]{3,2,1,0:T(8,128)S(1)}, f32[3,1,16,64]{3,2,1,0:T(8,128)S(1)}, u32[]{:S(2)}, u32[]{:S(2)}) collective-permute-start(f32[3,1,16,64]{3,2,1,0:T(8,128)S(1)} %get-tuple-element.244), channel_id=1, source_target_pairs={{1,0},{2,1},{3,2},{4,3},{5,4},{6,5},{7,6},{8,7},{9,8},{10,9},{11,1... | collective-permute-start | bytes 36872 | tf_op jit(solution)/shard_map/ppermute | solution.py:19
  68.9 12.9 %collective-permute-start.39 = (f32[3,1,16,64]{3,2,1,0:T(8,128)S(1)}, f32[3,1,16,64]{3,2,1,0:T(8,128)S(1)}, u32[]{:S(2)}, u32[]{:S(2)}) collective-permute-start(f32[3,1,16,64]{3,2,1,0:T(8,128)S(1)} %get-tuple-element.241), channel_id=1, source_target_pairs={{0,1},{1,2},{2,3},{3,4},{4,5},{5,6},{6,7},{7,8},{8,9},{9,10},{10,1... | collective-permute-start | bytes 36872 | tf_op jit(solution)/shard_map/ppermute | solution.py:16
  73.9 22.2 %collective-permute-start.1 = (f32[3,1,32,128]{2,3,1,0:T(8,128)}, f32[3,1,32,128]{2,3,1,0:T(8,128)S(1)}, u32[]{:S(2)}, u32[]{:S(2)}) collective-permute-start(f32[3,1,32,128]{2,3,1,0:T(8,128)} %get-tuple-element.141), channel_id=1, source_target_pairs={{1,0},{2,1},{3,2},{4,3},{5,4},{6,5},{7,6},{8,7},{9,8},{10,9},{11,1... | collective-permute-start | bytes 147464 | tf_op jit(solution)/shard_map/ppermute | solution.py:19
  75.2 20.5 %collective-permute-start.2 = (f32[3,1,32,128]{2,3,1,0:T(8,128)}, f32[3,1,32,128]{2,3,1,0:T(8,128)S(1)}, u32[]{:S(2)}, u32[]{:S(2)}) collective-permute-start(f32[3,1,32,128]{2,3,1,0:T(8,128)} %get-tuple-element.142), channel_id=1, source_target_pairs={{0,1},{1,2},{2,3},{3,4},{4,5},{5,6},{6,7},{7,8},{8,9},{9,10},{10,1... | collective-permute-start | bytes 147464 | tf_op jit(solution)/shard_map/ppermute | solution.py:16
  80.6 7.9 %collective-permute-start.38 = (f32[3,1,16,64]{3,2,1,0:T(8,128)S(1)}, f32[3,1,16,64]{3,2,1,0:T(8,128)S(1)}, u32[]{:S(2)}, u32[]{:S(2)}) collective-permute-start(f32[3,1,16,64]{3,2,1,0:T(8,128)S(1)} %get-tuple-element.240), channel_id=1, source_target_pairs={{1,0},{2,1},{3,2},{4,3},{5,4},{6,5},{7,6},{8,7},{9,8},{10,9},{11,1... | collective-permute-start | bytes 36872 | tf_op jit(solution)/shard_map/ppermute | solution.py:19
  89.3 8.0 %collective-permute-start.40 = (f32[3,1,16,64]{3,2,1,0:T(8,128)S(1)}, f32[3,1,16,64]{3,2,1,0:T(8,128)S(1)}, u32[]{:S(2)}, u32[]{:S(2)}) collective-permute-start(f32[3,1,16,64]{3,2,1,0:T(8,128)S(1)} %get-tuple-element.238), channel_id=1, source_target_pairs={{1,0},{2,1},{3,2},{4,3},{5,4},{6,5},{7,6},{8,7},{9,8},{10,9},{11,1... | collective-permute-start | bytes 36872 | tf_op jit(solution)/shard_map/ppermute | solution.py:19
  99.8 10.5 %collective-permute-start.4 = (f32[3,1,32,128]{2,3,1,0:T(8,128)S(1)}, f32[3,1,32,128]{2,3,1,0:T(8,128)S(1)}, u32[]{:S(2)}, u32[]{:S(2)}) collective-permute-start(f32[3,1,32,128]{2,3,1,0:T(8,128)S(1)} %get-tuple-element.139), channel_id=1, source_target_pairs={{1,0},{2,1},{3,2},{4,3},{5,4},{6,5},{7,6},{8,7},{9,8},{10,9},{11,1... | collective-permute-start | bytes 147464 | tf_op jit(solution)/shard_map/ppermute | solution.py:19
  101.1 8.7 %collective-permute-start.5 = (f32[3,1,32,128]{2,3,1,0:T(8,128)S(1)}, f32[3,1,32,128]{2,3,1,0:T(8,128)S(1)}, u32[]{:S(2)}, u32[]{:S(2)}) collective-permute-start(f32[3,1,32,128]{2,3,1,0:T(8,128)S(1)} %get-tuple-element.140), channel_id=1, source_target_pairs={{0,1},{1,2},{2,3},{3,4},{4,5},{5,6},{6,7},{7,8},{8,9},{9,10},{10,1... | collective-permute-start | bytes 147464 | tf_op jit(solution)/shard_map/ppermute | solution.py:16
  133.2 13.8 %collective-permute-start.7 = (f32[3,1,16,64]{3,2,1,0:T(8,128)S(1)}, f32[3,1,16,64]{3,2,1,0:T(8,128)S(1)}, u32[]{:S(2)}, u32[]{:S(2)}) collective-permute-start(f32[3,1,16,64]{3,2,1,0:T(8,128)S(1)} %get-tuple-element.259), channel_id=1, source_target_pairs={{0,1},{1,2},{2,3},{3,4},{4,5},{5,6},{6,7},{7,8},{8,9},{9,10},{10,1... | collective-permute-start | bytes 36872 | tf_op jit(solution)/shard_map/ppermute | solution.py:16
  138.5 14.1 %collective-permute-start.42 = (f32[3,1,16,64]{3,2,1,0:T(8,128)S(1)}, f32[3,1,16,64]{3,2,1,0:T(8,128)S(1)}, u32[]{:S(2)}, u32[]{:S(2)}) collective-permute-start(f32[3,1,16,64]{3,2,1,0:T(8,128)S(1)} %get-tuple-element.235), channel_id=1, source_target_pairs={{1,0},{2,1},{3,2},{4,3},{5,4},{6,5},{7,6},{8,7},{9,8},{10,9},{11,1... | collective-permute-start | bytes 36872 | tf_op jit(solution)/shard_map/ppermute | solution.py:19
  139.8 12.7 %collective-permute-start.43 = (f32[3,1,16,64]{3,2,1,0:T(8,128)S(1)}, f32[3,1,16,64]{3,2,1,0:T(8,128)S(1)}, u32[]{:S(2)}, u32[]{:S(2)}) collective-permute-start(f32[3,1,16,64]{3,2,1,0:T(8,128)S(1)} %get-tuple-element.236), channel_id=1, source_target_pairs={{0,1},{1,2},{2,3},{3,4},{4,5},{5,6},{6,7},{7,8},{8,9},{9,10},{10,1... | collective-permute-start | bytes 36872 | tf_op jit(solution)/shard_map/ppermute | solution.py:16
  154.1 7.7 %collective-permute-start.9 = (f32[3,1,16,64]{3,2,1,0:T(8,128)S(1)}, f32[3,1,16,64]{3,2,1,0:T(8,128)S(1)}, u32[]{:S(2)}, u32[]{:S(2)}) collective-permute-start(f32[3,1,16,64]{3,2,1,0:T(8,128)S(1)} %get-tuple-element.257), channel_id=1, source_target_pairs={{0,1},{1,2},{2,3},{3,4},{4,5},{5,6},{6,7},{7,8},{8,9},{9,10},{10,1... | collective-permute-start | bytes 36872 | tf_op jit(solution)/shard_map/ppermute | solution.py:16
  160.3 7.5 %collective-permute-start.8 = (f32[3,1,16,64]{3,2,1,0:T(8,128)S(1)}, f32[3,1,16,64]{3,2,1,0:T(8,128)S(1)}, u32[]{:S(2)}, u32[]{:S(2)}) collective-permute-start(f32[3,1,16,64]{3,2,1,0:T(8,128)S(1)} %get-tuple-element.256), channel_id=1, source_target_pairs={{1,0},{2,1},{3,2},{4,3},{5,4},{6,5},{7,6},{8,7},{9,8},{10,9},{11,1... | collective-permute-start | bytes 36872 | tf_op jit(solution)/shard_map/ppermute | solution.py:19
  168.1 7.3 %collective-permute-start.11 = (f32[3,1,16,64]{3,2,1,0:T(8,128)S(1)}, f32[3,1,16,64]{3,2,1,0:T(8,128)S(1)}, u32[]{:S(2)}, u32[]{:S(2)}) collective-permute-start(f32[3,1,16,64]{3,2,1,0:T(8,128)S(1)} %get-tuple-element.255), channel_id=1, source_target_pairs={{0,1},{1,2},{2,3},{3,4},{4,5},{5,6},{6,7},{7,8},{8,9},{9,10},{10,1... | collective-permute-start | bytes 36872 | tf_op jit(solution)/shard_map/ppermute | solution.py:16
  183.0 8.9 %collective-permute-start.13 = (f32[3,1,32,128]{2,3,1,0:T(8,128)S(1)}, f32[3,1,32,128]{2,3,1,0:T(8,128)S(1)}, u32[]{:S(2)}, u32[]{:S(2)}) collective-permute-start(f32[3,1,32,128]{2,3,1,0:T(8,128)S(1)} %get-tuple-element.138), channel_id=1, source_target_pairs={{0,1},{1,2},{2,3},{3,4},{4,5},{5,6},{6,7},{7,8},{8,9},{9,10},{10,1... | collective-permute-start | bytes 147464 | tf_op jit(solution)/shard_map/ppermute | solution.py:16
  187.9 9.8 %collective-permute-start.12 = (f32[3,1,32,128]{2,3,1,0:T(8,128)S(1)}, f32[3,1,32,128]{2,3,1,0:T(8,128)S(1)}, u32[]{:S(2)}, u32[]{:S(2)}) collective-permute-start(f32[3,1,32,128]{2,3,1,0:T(8,128)S(1)} %get-tuple-element.137), channel_id=1, source_target_pairs={{1,0},{2,1},{3,2},{4,3},{5,4},{6,5},{7,6},{8,7},{9,8},{10,9},{11,1... | collective-permute-start | bytes 147464 | tf_op jit(solution)/shard_map/ppermute | solution.py:19
  200.6 9.3 %collective-permute-start.15 = (f32[3,1,32,128]{2,3,1,0:T(8,128)S(1)}, f32[3,1,32,128]{2,3,1,0:T(8,128)S(1)}, u32[]{:S(2)}, u32[]{:S(2)}) collective-permute-start(f32[3,1,32,128]{2,3,1,0:T(8,128)S(1)} %get-tuple-element.136), channel_id=1, source_target_pairs={{0,1},{1,2},{2,3},{3,4},{4,5},{5,6},{6,7},{7,8},{8,9},{9,10},{10,1... | collective-permute-start | bytes 147464 | tf_op jit(solution)/shard_map/ppermute | solution.py:16
  204.7 7.8 %collective-permute-start.14 = (f32[3,1,32,128]{2,3,1,0:T(8,128)S(1)}, f32[3,1,32,128]{2,3,1,0:T(8,128)S(1)}, u32[]{:S(2)}, u32[]{:S(2)}) collective-permute-start(f32[3,1,32,128]{2,3,1,0:T(8,128)S(1)} %get-tuple-element.135), channel_id=1, source_target_pairs={{1,0},{2,1},{3,2},{4,3},{5,4},{6,5},{7,6},{8,7},{9,8},{10,9},{11,1... | collective-permute-start | bytes 147464 | tf_op jit(solution)/shard_map/ppermute | solution.py:19
  218.1 7.8 %collective-permute-start.16 = (f32[3,1,32,128]{2,3,1,0:T(8,128)S(1)}, f32[3,1,32,128]{2,3,1,0:T(8,128)S(1)}, u32[]{:S(2)}, u32[]{:S(2)}) collective-permute-start(f32[3,1,32,128]{2,3,1,0:T(8,128)S(1)} %get-tuple-element.133), channel_id=1, source_target_pairs={{1,0},{2,1},{3,2},{4,3},{5,4},{6,5},{7,6},{8,7},{9,8},{10,9},{11,1... | collective-permute-start | bytes 147464 | tf_op jit(solution)/shard_map/ppermute | solution.py:19
  227.8 7.3 %collective-permute-start.19 = (f32[3,1,32,128]{2,3,1,0:T(8,128)S(1)}, f32[3,1,32,128]{2,3,1,0:T(8,128)S(1)}, u32[]{:S(2)}, u32[]{:S(2)}) collective-permute-start(f32[3,1,32,128]{2,3,1,0:T(8,128)S(1)} %get-tuple-element.132), channel_id=1, source_target_pairs={{0,1},{1,2},{2,3},{3,4},{4,5},{5,6},{6,7},{7,8},{8,9},{9,10},{10,1... | collective-permute-start | bytes 147464 | tf_op jit(solution)/shard_map/ppermute | solution.py:16
  231.9 7.6 %collective-permute-start.18 = (f32[3,1,32,128]{2,3,1,0:T(8,128)S(1)}, f32[3,1,32,128]{2,3,1,0:T(8,128)S(1)}, u32[]{:S(2)}, u32[]{:S(2)}) collective-permute-start(f32[3,1,32,128]{2,3,1,0:T(8,128)S(1)} %get-tuple-element.131), channel_id=1, source_target_pairs={{1,0},{2,1},{3,2},{4,3},{5,4},{6,5},{7,6},{8,7},{9,8},{10,9},{11,1... | collective-permute-start | bytes 147464 | tf_op jit(solution)/shard_map/ppermute | solution.py:19
  241.4 7.8 %collective-permute-start.21 = (f32[3,1,32,128]{2,3,1,0:T(8,128)S(1)}, f32[3,1,32,128]{2,3,1,0:T(8,128)S(1)}, u32[]{:S(2)}, u32[]{:S(2)}) collective-permute-start(f32[3,1,32,128]{2,3,1,0:T(8,128)S(1)} %get-tuple-element.130), channel_id=1, source_target_pairs={{0,1},{1,2},{2,3},{3,4},{4,5},{5,6},{6,7},{7,8},{8,9},{9,10},{10,1... | collective-permute-start | bytes 147464 | tf_op jit(solution)/shard_map/ppermute | solution.py:16
  246.0 7.6 %collective-permute-start.20 = (f32[3,1,32,128]{2,3,1,0:T(8,128)S(1)}, f32[3,1,32,128]{2,3,1,0:T(8,128)S(1)}, u32[]{:S(2)}, u32[]{:S(2)}) collective-permute-start(f32[3,1,32,128]{2,3,1,0:T(8,128)S(1)} %get-tuple-element.129), channel_id=1, source_target_pairs={{1,0},{2,1},{3,2},{4,3},{5,4},{6,5},{7,6},{8,7},{9,8},{10,9},{11,1... | collective-permute-start | bytes 147464 | tf_op jit(solution)/shard_map/ppermute | solution.py:19
  278.6 12.8 %collective-permute-start.23 = (f32[3,1,16,64]{3,2,1,0:T(8,128)S(1)}, f32[3,1,16,64]{3,2,1,0:T(8,128)S(1)}, u32[]{:S(2)}, u32[]{:S(2)}) collective-permute-start(f32[3,1,16,64]{3,2,1,0:T(8,128)S(1)} %get-tuple-element.253), channel_id=1, source_target_pairs={{0,1},{1,2},{2,3},{3,4},{4,5},{5,6},{6,7},{7,8},{8,9},{9,10},{10,1... | collective-permute-start | bytes 36872 | tf_op jit(solution)/shard_map/ppermute | solution.py:16
  284.3 12.4 %collective-permute-start.44 = (f32[3,1,16,64]{3,2,1,0:T(8,128)S(1)}, f32[3,1,16,64]{3,2,1,0:T(8,128)S(1)}, u32[]{:S(2)}, u32[]{:S(2)}) collective-permute-start(f32[3,1,16,64]{3,2,1,0:T(8,128)S(1)} %get-tuple-element.232), channel_id=1, source_target_pairs={{1,0},{2,1},{3,2},{4,3},{5,4},{6,5},{7,6},{8,7},{9,8},{10,9},{11,1... | collective-permute-start | bytes 36872 | tf_op jit(solution)/shard_map/ppermute | solution.py:19
  322.4 10.1 %collective-permute-start.29 = (f32[3,1,32,128]{2,3,1,0:T(8,128)S(1)}, f32[3,1,32,128]{2,3,1,0:T(8,128)S(1)}, u32[]{:S(2)}, u32[]{:S(2)}) collective-permute-start(f32[3,1,32,128]{2,3,1,0:T(8,128)S(1)} %get-tuple-element.128), channel_id=1, source_target_pairs={{0,1},{1,2},{2,3},{3,4},{4,5},{5,6},{6,7},{7,8},{8,9},{9,10},{10,1... | collective-permute-start | bytes 147464 | tf_op jit(solution)/shard_map/ppermute | solution.py:16
  328.1 7.6 %collective-permute-start.28 = (f32[3,1,32,128]{2,3,1,0:T(8,128)S(1)}, f32[3,1,32,128]{2,3,1,0:T(8,128)S(1)}, u32[]{:S(2)}, u32[]{:S(2)}) collective-permute-start(f32[3,1,32,128]{2,3,1,0:T(8,128)S(1)} %get-tuple-element.127), channel_id=1, source_target_pairs={{1,0},{2,1},{3,2},{4,3},{5,4},{6,5},{7,6},{8,7},{9,8},{10,9},{11,1... | collective-permute-start | bytes 147464 | tf_op jit(solution)/shard_map/ppermute | solution.py:19
  337.4 7.3 %collective-permute-start.31 = (f32[3,1,32,128]{2,3,1,0:T(8,128)S(1)}, f32[3,1,32,128]{2,3,1,0:T(8,128)S(1)}, u32[]{:S(2)}, u32[]{:S(2)}) collective-permute-start(f32[3,1,32,128]{2,3,1,0:T(8,128)S(1)} %get-tuple-element.126), channel_id=1, source_target_pairs={{0,1},{1,2},{2,3},{3,4},{4,5},{5,6},{6,7},{7,8},{8,9},{9,10},{10,1... | collective-permute-start | bytes 147464 | tf_op jit(solution)/shard_map/ppermute | solution.py:16
  342.9 7.6 %collective-permute-start.30 = (f32[3,1,32,128]{2,3,1,0:T(8,128)S(1)}, f32[3,1,32,128]{2,3,1,0:T(8,128)S(1)}, u32[]{:S(2)}, u32[]{:S(2)}) collective-permute-start(f32[3,1,32,128]{2,3,1,0:T(8,128)S(1)} %get-tuple-element.125), channel_id=1, source_target_pairs={{1,0},{2,1},{3,2},{4,3},{5,4},{6,5},{7,6},{8,7},{9,8},{10,9},{11,1... | collective-permute-start | bytes 147464 | tf_op jit(solution)/shard_map/ppermute | solution.py:19
  (41 other events, 376.4 us)
where the time goes:
time: 401 us; the launch traced here: 399 us
  starting transfers between devices  145 us (36%)
  waiting for transfers between devices  90.2 us (22%)
  local copies, waits for them, and re-layouts  60.3 us (15%)
  other arithmetic  58.7 us (15%)
  blocking collectives  40.5 us (10%)
  between operations  4.05 us (1%)
    ppermute x22, starting transfers between devices, extended(): lax.ppermute(lax.slice_in_dim(block, block.shape[dim] - width, None, axis...  108 us
    ppermute x22, waiting for transfers between devices, extended(): lax.ppermute(lax.slice_in_dim(block, 0, width, axis=dim), axis, backward)  68.1 us
    reshape x3, local copies, waits for them, and re-layouts, restrict_vector(): values.reshape(shape[0], shape[1] // 2, 2, shape[2] // 2, 2, shape[3] //...  42.4 us
    psum x1, blocking collectives, body(): lax.psum((jnp.sum(force * iterate), jnp.sum(coarse_force * coarse_field))...  40.5 us
    ppermute x22, starting transfers between devices, extended(): lax.ppermute(lax.slice_in_dim(block, 0, width, axis=dim), axis, backward)  28.8 us
    ppermute x22, waiting for transfers between devices, extended(): lax.ppermute(lax.slice_in_dim(block, block.shape[dim] - width, None, axis...  22.1 us
    reduce_sum x3, other arithmetic, restrict_vector(): values.reshape(shape[0], shape[1] // 2, 2, shape[2] // 2, 2, shape[3] //...  16.6 us
    ppermute x2, starting transfers between devices, from_behind(): return lax.ppermute(x, axis, pairs)  8.27 us
  transfers between devices with their start and end apart: 46, of which 31 were waited for; matrix products, arithmetic and copies ran while one was open for 8% of the time, Pallas kernels for 0%

commit v1 on v0

v1 whole, which is shorter than its diff:
```python
import functools

import jax
import jax.numpy as jnp
from jax import lax
from jax.experimental import pallas as pl
from jax.experimental.pallas import tpu as pltpu
from jax.sharding import PartitionSpec as P

CDEG = 4
FINE = (0.25, 2.0)
COARSE = (0.02, 2.0)
H = 8
U_FINE = 1
U_COARSE = 1


def coefficients(low, high, degree):
    centre, half = (high + low) / 2.0, (high - low) / 2.0
    ratio = centre / half
    rho = 1.0 / ratio
    steps = []
    for _ in range(degree - 1):
        nxt = 1.0 / (2.0 * ratio - rho)
        steps.append((nxt * rho, 2.0 * nxt / half))
        rho = nxt
    return 1.0 / centre, steps


def shifts(rows, lanes, step):
    lane = lax.broadcasted_iota(jnp.int32, (rows, lanes), 1)
    row = lax.broadcasted_iota(jnp.int32, (rows, lanes), 0)

    def ahead_x(u):
        return jnp.where(lane < lanes - step, pltpu.roll(u, lanes - step, 1), 0.0)

    def back_x(u):
        return jnp.where(lane >= step, pltpu.roll(u, step, 1), 0.0)

    def ahead_y(u):
        return jnp.where(row < rows - 1, pltpu.roll(u, rows - 1, 0), 0.0)

    def back_y(u):
        return jnp.where(row >= 1, pltpu.roll(u, 1, 0), 0.0)

    return ahead_x, back_x, ahead_y, back_y


def loop(lo, hi, body, carry, unroll):
    return lax.fori_loop(lo + H, hi + H, body, carry, unroll=unroll)


def invert(lam, inv, lo, hi, first, last, sh, unroll):
    _, back_x, _, back_y = sh

    def body(z, below):
        m = lam[z]
        mx, my = back_x(m), back_y(m)
        base = (m + below) + (m + my) + (m + mx) + m
        live = jnp.logical_and(z - H >= first, z - H < last)
        for c, extra in enumerate((mx, my, below)):
            inv[c, z] = jnp.where(live, 1.0 / (base + extra), 0.0)
        return m

    loop(lo, hi, body, lam[lo - 1 + H], unroll)


def begin(src, inv, w, x, lo, hi, scale, unroll):
    def body(z, carry):
        for c in range(3):
            v = inv[c, z] * src[c, z] * scale
            w[c, z] = v
            if x is not None:
                x[c, z] = v
        return carry

    loop(lo, hi, body, 0, unroll)


def sweep(src, r, w, x, lam, inv, lo, hi, old, new, sh, unroll):
    ahead_x, back_x, ahead_y, back_y = sh

    def upward(z, u, div):
        m = lam[z]
        gz = [w[c, z + 1] - u[c] for c in range(3)]
        s = m * (div + gz[2])
        return [m * gz[0], m * gz[1], m * gz[2] + s], s, m

    def spread(u):
        return (ahead_x(u[0]) - u[0]) + (ahead_y(u[1]) - u[1])

    def body(z, below):
        u = [w[c, z] for c in range(3)]
        gx = [ahead_x(v) - v for v in u]
        gy = [ahead_y(v) - v for v in u]
        up, s, m = upward(z, u, gx[0] + gy[1])
        fx = [m * g for g in gx]
        fy = [m * g for g in gy]
        fx[0] = fx[0] + s
        fy[1] = fy[1] + s
        for c in range(3):
            a = (below[c] - up[c]) + (back_y(fy[c]) - fy[c]) + (back_x(fx[c]) - fx[c])
            rest = src[c, z] - a
            r[c, z] = rest
            if new is not None:
                v = new * (inv[c, z] * rest)
                if old is not None:
                    v = old * u[c] + v
                w[c, z] = v
                if x is not None:
                    x[c, z] = x[c, z] + v
        return tuple(up)

    z0 = lo - 1 + H
    u0 = [w[c, z0] for c in range(3)]
    up0, _, _ = upward(z0, u0, spread(u0))
    loop(lo, hi, body, tuple(up0), unroll)


def pack(load, tmp, scale, even):
    lanes = even.shape[1]
    halves = []
    for k in range(2):
        tmp[k] = load(2 * k) + load(2 * k + 1)
        n = even.shape[0]
        halves.append(tmp[k, pl.ds(0, n, stride=2), :] + tmp[k, pl.ds(1, n, stride=2), :])
    a, b = halves
    return scale * jnp.where(even, a + pltpu.roll(a, lanes - 1, 1), b + pltpu.roll(b, 1, 1))


def unpack(p, even):
    lanes = even.shape[1]
    return jnp.where(even, p, pltpu.roll(p, 1, 1)), jnp.where(even, pltpu.roll(p, lanes - 1, 1), p)


def kernel(n, L, force, modulus, out, cout, comp, fm, lam, inv, r, w, x, tmp, cg, c1, c2, clam, cinv, cf, cr, cw, ce, part, lsem, ssem, rsem, sums_s, sums_r):
    me = lax.axis_index("slab")
    rows, lanes = fm.shape[2], fm.shape[3]
    crows = rows // 2
    barrier = pltpu.get_barrier_semaphore()

    def greet(k, carry):
        pl.semaphore_signal(barrier, inc=1, device_id={"slab": lax.rem(me + k, n)}, device_id_type=pl.DeviceIdType.MESH)
        return carry

    lax.fori_loop(1, n, greet, 0)
    own = pl.ds(H, L)
    loads = [
        pltpu.make_async_copy(force, fm.at[pl.ds(0, 3), own], lsem.at[0]),
        pltpu.make_async_copy(modulus, fm.at[3, own], lsem.at[1]),
    ]
    for cp in loads:
        cp.start()

    copies = {}

    def remote(name, src, dst, d):
        i = len(copies)
        copies[name] = (
            pltpu.make_async_remote_copy(
                src_ref=src, dst_ref=dst, send_sem=ssem.at[i], recv_sem=rsem.at[i],
                device_id={"slab": me + d}, device_id_type=pl.DeviceIdType.MESH,
            ),
            d, dst,
        )

    def inside(i):
        return jnp.logical_and(i >= 0, i < n)

    def start(name):
        cp, d, _ = copies[name]
        pl.when(inside(me + d))(cp.start)

    def wait(name):
        cp, d, _ = copies[name]
        pl.when(inside(me - d))(cp.wait_recv)

    def clear(name):
        _, d, dst = copies[name]

        @pl.when(jnp.logical_not(inside(me - d)))
        def _():
            dst[...] = jnp.zeros(dst.shape, jnp.float32)

    def layers(name, d, lo, hi):
        mine = fm.at[:, pl.ds(H + lo, hi - lo)]
        theirs = fm.at[:, pl.ds(H + lo - d * L, hi - lo)]
        remote(name, mine, theirs, d)

    layers("near+", 1, 1, L)
    layers("near-", -1, 0, 2)
    layers("next+", 1, 0, 1)
    layers("next-", -1, 2, L)
    layers("far+", 2, 0, L)
    layers("far-", -2, 0, L - 1)
    for name, buf, reach in (("g", cg, 4), ("c1", c1, 3), ("c2", c2, 2)):
        for k in range(1, reach + 1):
            for d in (k, -k):
                remote((name, d), buf.at[reach], buf.at[reach - d], d)

    for name in copies:
        clear(name)

    even = lax.rem(lax.broadcasted_iota(jnp.int32, (crows, lanes), 1), 2) == 0
    fsh = shifts(rows, lanes, 1)
    csh = shifts(crows, lanes, 2)
    fscale, ((fold, fnew),) = coefficients(*FINE, 2)
    cscale, csteps = coefficients(*COARSE, CDEG)
    _, wsteps = coefficients(*COARSE, 2 * CDEG)

    for cp in loads:
        cp.wait()
    pl.semaphore_wait(barrier, n - 1)
    for name in ("near+", "near-"):
        start(name)
    for c in range(4):
        cg[4, c] = pack(lambda z: fm[c, H + z], tmp, 0.5 if c < 3 else 0.05, even)
    for k in range(1, 5):
        start(("g", k))
        start(("g", -k))
    for name in ("far+", "far-", "next+", "next-"):
        start(name)

    def take(lo, hi):
        def body(z, carry):
            lam[z] = 0.4 * fm[3, z]
            return carry

        loop(lo, hi, body, 0, U_FINE)

    first, last = -me * L, (n - me) * L
    cfirst, clast = -me * (L // 2), (n - me) * (L // 2)

    def exchange(name, buf, reach):
        for c in range(3):
            buf[reach, c] = pack(lambda z: r[c, H + z], tmp, 0.5, even)
        for k in range(1, reach + 1):
            start((name, k))
            start((name, -k))

    def gather(name, buf, reach, into):
        for k in range(1, reach + 1):
            wait((name, k))
            wait((name, -k))
        for d in range(-reach, reach + 1):
            for c in range(3):
                a, b = unpack(buf[reach + d, c], even)
                into[c, H + 2 * d] = a
                into[c, H + 2 * d + 1] = b

    wait("near+")
    wait("near-")
    take(-3, L + 2)
    invert(lam, inv, -2, L + 2, first, last, fsh, U_FINE)
    begin(fm, inv, w, None, -2, L + 2, fscale, U_FINE)
    sweep(fm, r, w, None, lam, inv, -1, L + 1, fold, fnew, fsh, U_FINE)
    sweep(r, r, w, None, lam, inv, 0, L, None, None, fsh, U_FINE)
    exchange("c1", c1, 3)

    for k in range(1, 5):
        wait(("g", k))
        wait(("g", -k))
    for d in range(-4, 5):
        for c in range(4):
            a, b = unpack(cg[4 + d, c], even)
            for z, v in ((H + 2 * d, a), (H + 2 * d + 1, b)):
                if c < 3:
                    cf[c, z] = v
                else:
                    clam[z] = v
    invert(clam, cinv, -7, 9, cfirst, clast, csh, U_COARSE)
    for name in ("far+", "far-", "next+", "next-"):
        wait(name)
    take(-8, -3)
    take(L + 2, L + 7)
    invert(lam, inv, -7, -2, first, last, fsh, U_FINE)
    invert(lam, inv, L + 2, L + 7, first, last, fsh, U_FINE)
    begin(fm, inv, w, x, -7, L + 7, fscale, U_FINE)
    sweep(fm, r, w, x, lam, inv, -6, L + 6, fold, fnew, fsh, U_FINE)
    sweep(r, r, w, None, lam, inv, -5, L + 5, None, None, fsh, U_FINE)

    def solve(lo, hi, rhs, steps):
        begin(rhs, cinv, cw, ce, lo, hi, cscale, U_COARSE)
        for k, (old, new) in enumerate(steps):
            src = rhs if k == 0 else cr
            sweep(src, cr, cw, ce, clam, cinv, lo + k + 1, hi - k - 1, old, new, csh, U_COARSE)

    def prolong(lo, hi):
        def body(z, carry):
            for c in range(3):
                e = ce[c, z]
                for half in range(2):
                    f = 2 * (z - H) + half + H
                    w[c, f, pl.ds(0, crows, stride=2), :] = e
                    w[c, f, pl.ds(1, crows, stride=2), :] = e
                    x[c, f] = x[c, f] + w[c, f]
            return carry

        loop(lo, hi, body, 0, U_COARSE)

    gather("c1", c1, 3, cr)
    solve(-6, 8, cr, csteps)
    prolong(-3, 5)
    sweep(r, r, w, x, lam, inv, -5, L + 5, None, fscale, fsh, U_FINE)
    sweep(r, r, w, x, lam, inv, -4, L + 4, fold, fnew, fsh, U_FINE)
    sweep(r, r, w, x, lam, inv, -3, L + 3, None, fscale, fsh, U_FINE)
    sweep(r, r, w, x, lam, inv, -2, L + 2, fold, fnew, fsh, U_FINE)
    sweep(r, r, w, None, lam, inv, -1, L + 1, None, None, fsh, U_FINE)
    exchange("c2", c2, 2)

    solve(-7, 9, cf, wsteps)
    coarse_sum = jnp.zeros((crows, lanes), jnp.float32)
    pick = (
        lax.broadcasted_iota(jnp.int32, (lanes, lanes // 2), 0)
        == 2 * lax.broadcasted_iota(jnp.int32, (lanes, lanes // 2), 1)
    ).astype(jnp.float32)
    for c in range(3):
        for z in range(L // 2):
            v = ce[c, H + z]
            coarse_sum = coarse_sum + v * cf[c, H + z]
            cout[c, z] = jnp.dot(v, pick, precision=lax.Precision.HIGHEST, preferred_element_type=jnp.float32)

    gather("c2", c2, 2, cr)
    solve(-4, 6, cr, csteps)
    prolong(-1, 3)
    sweep(r, r, w, x, lam, inv, -1, L + 1, None, fscale, fsh, U_FINE)
    sweep(r, r, w, x, lam, inv, 0, L, fold, fnew, fsh, U_FINE)

    fine_sum = jnp.zeros((rows, lanes), jnp.float32)
    for c in range(3):
        for z in range(L):
            v = x[c, H + z]
            out[c, z] = v
            fine_sum = fine_sum + v * fm[c, H + z]
    part[0, 0:1] = jnp.sum(fine_sum, axis=0, keepdims=True)
    part[0, 1:2] = jnp.sum(coarse_sum, axis=0, keepdims=True)

    def tell(k):
        return pltpu.make_async_remote_copy(
            src_ref=part.at[0], dst_ref=part.at[k], send_sem=sums_s.at[k], recv_sem=sums_r.at[k],
            device_id={"slab": lax.rem(me + k, n)}, device_id_type=pl.DeviceIdType.MESH,
        )

    def say(k, carry):
        tell(k).start()
        return carry

    def hear(k, carry):
        tell(k).wait_recv()
        return carry

    lax.fori_loop(1, n, say, 0)
    for name in copies:
        cp, d, _ = copies[name]
        pl.when(inside(me + d))(cp.wait_send)
    lax.fori_loop(1, n, hear, 0)
    total = jnp.sum(part[...], axis=0)
    cells = 1.0 / (n * L * rows * lanes)
    comp[0] = jnp.sum(total[0:1]) * cells
    comp[1] = jnp.sum(total[1:2]) * cells

    def done(k, carry):
        tell(k).wait_send()
        return carry

    lax.fori_loop(1, n, done, 0)


def body(n, force, modulus):
    _, L, rows, lanes = force.shape
    f32 = jnp.float32
    fine, coarse = (L + 2 * H, rows, lanes), (L // 2 + 2 * H, rows // 2, lanes)
    pair = (rows // 2, lanes)
    V = pltpu.VMEM
    remotes = 6 + 8 + 6 + 4
    scratch = [
        V((4,) + fine, f32), V(fine, f32), V((3,) + fine, f32), V((3,) + fine, f32),
        V((3,) + fine, f32), V((3,) + fine, f32), V((2, rows, lanes), f32),
        V((9, 4) + pair, f32), V((7, 3) + pair, f32), V((5, 3) + pair, f32),
        V(coarse, f32), V((3,) + coarse, f32), V((3,) + coarse, f32), V((3,) + coarse, f32),
        V((3,) + coarse, f32), V((3,) + coarse, f32), V((n, 2, lanes), f32),
        pltpu.SemaphoreType.DMA((2,)),
        pltpu.SemaphoreType.DMA((remotes,)), pltpu.SemaphoreType.DMA((remotes,)),
        pltpu.SemaphoreType.DMA((n,)), pltpu.SemaphoreType.DMA((n,)),
    ]
    vmem = pl.BlockSpec(memory_space=pltpu.VMEM)
    return pl.pallas_call(
        functools.partial(kernel, n, L),
        out_shape=(
            jax.ShapeDtypeStruct(force.shape, f32),
            jax.ShapeDtypeStruct((3, L // 2, rows // 2, lanes // 2), f32),
            jax.ShapeDtypeStruct((2,), f32),
        ),
        in_specs=[pl.BlockSpec(memory_space=pl.ANY)] * 2,
        out_specs=(vmem, vmem, pl.BlockSpec(memory_space=pltpu.SMEM)),
        scratch_shapes=scratch,
        compiler_params=pltpu.CompilerParams(collective_id=0, has_side_effects=True),
    )(force, modulus)


def solution(mesh):
    return jax.shard_map(
        functools.partial(body, mesh.shape["slab"]),
        mesh=mesh,
        in_specs=(P(None, "slab", None, "sample"), P("slab", None, "sample")),
        out_specs=(P(None, "slab", None, "sample"), P(None, "slab", None, "sample"), P("sample")),
        check_vma=False,
    )
```

time: 401 us -> 71.5 us (0.18)
  starting transfers between devices: 145 us -> 0 us
  waiting for transfers between devices: 90.2 us -> 0 us
  Pallas kernels: 0 us -> 67.9 us
  other arithmetic: 58.7 us -> 0 us
  local copies, waits for them, and re-layouts: 60.3 us -> 2.77 us
  blocking collectives: 40.5 us -> 0 us
    ppermute x46 -> x0, starting transfers between devices: 145 us -> none  [the longest x22 108 us: extended(): lax.ppermute(lax.slice_in_dim(block, block.shape[dim] - width, None, axis...]
    ppermute x46 -> x0, waiting for transfers between devices: 90.2 us -> none  [the longest x22 68.1 us: extended(): lax.ppermute(lax.slice_in_dim(block, 0, width, axis=dim), axis, backward)]
    pallas_call x0 -> x1, Pallas kernels: none -> 67.9 us  [body(): pl.pallas_call(functools.partial(kernel, n, L), out_shape=(jax.ShapeDtype...]
    reshape x6 -> x0, local copies, waits for them, and re-layouts: 49.8 us -> none  [the longest x3 42.4 us: restrict_vector(): values.reshape(shape[0], shape[1] // 2, 2, shape[2] // 2, 2, shape[3] //...]
    psum x1 -> x0, blocking collectives: 40.5 us -> none  [body(): lax.psum((jnp.sum(force * iterate), jnp.sum(coarse_force * coarse_field))...]
    reduce_sum x6 -> x0, other arithmetic: 23.5 us -> none  [the longest x3 16.6 us: restrict_vector(): values.reshape(shape[0], shape[1] // 2, 2, shape[2] // 2, 2, shape[3] //...]
    mul x52 -> x0, other arithmetic: 10.2 us -> none  [the longest x11 5.03 us: operate_extended(): flux_z = lame_ext * grad_z]
    add x15 -> x0, other arithmetic: 6.87 us -> none  [the longest x13 6.68 us: chebyshev(): rho_next * rho_now * update]
  transfers between devices with their start and end apart: 46 -> 0, of which waited for: 31 -> 0; matrix products, arithmetic and copies ran while one was open for 8% -> 0% of each run, Pallas kernels for 0% -> 0%
where the time goes in v1:
time: 71.5 us; the launch traced here: 71.3 us
  Pallas kernels  67.9 us (95%)
  local copies, waits for them, and re-layouts  2.77 us (4%)
    pallas_call x1, Pallas kernels, body(): pl.pallas_call(functools.partial(kernel, n, L), out_shape=(jax.ShapeDtype...  67.9 us
    unnamed x7, local copies, waits for them, and re-layouts  2.77 us

profile of v1, /device:TPU:0, one launch (start us, length us, event | category | flops | bytes accessed | tf_op | source)
XLA Modules:
  0.0 71.3 jit_solution(6976291708326679689)
XLA Ops:
  0.6 67.9 %shard_map.49 = (f32[3,4,32,128]{3,2,1,0:T(8,128)}, f32[3,2,16,64]{3,2,1,0:T(8,128)}, f32[2]{0:T(128)}) custom-call(f32[3,4,32,128]{3,2,1,0:T(8,128)} %force.1, f32[4,32,128]{2,1,0:T(8,128)} %modulus.1), custom_call_target="tpu_custom_call" | custom-call | tf_op jit(solution)/shard_map/pallas_call | solution.py:387
  68.6 0.0 copy-start
  68.6 1.6 %copy.8 = f32[3,4,32,128]{3,2,1,0:T(8,128)} copy(f32[3,4,32,128]{3,2,1,0:T(8,128)} %get-tuple-element.6) | data formatting | bytes 393216
  70.2 0.0 copy-done
  70.2 0.0 copy-start.1
  70.2 0.6 copy.9
  70.8 0.0 copy-done.1
  70.8 0.5 copy.10
Async XLA Ops:
  68.6 1.6 %copy-start = (f32[3,2,16,64]{3,2,1,0:T(8,128)S(1)}, f32[3,2,16,64]{3,2,1,0:T(8,128)}, u32[]{:S(2)}) copy-start(f32[3,2,16,64]{3,2,1,0:T(8,128)} %get-tuple-element.7) | copy-start | bytes 73732
  70.2 0.6 copy-start.1

commit v2 on v1

--- a/solution.py
+++ b/solution.py
@@ -11,8 +11,16 @@
 FINE = (0.25, 2.0)
 COARSE = (0.02, 2.0)
 H = 8
-U_FINE = 1
-U_COARSE = 1
+REACH = 4
+U_FINE = True
+U_COARSE = True
+
+
+def rounds(n):
+    count = 0
+    while REACH * 2**count < n - 1:
+        count += 1
+    return count
 
 
 def coefficients(low, high, degree):
@@ -133,17 +141,34 @@
     return jnp.where(even, p, pltpu.roll(p, 1, 1)), jnp.where(even, pltpu.roll(p, lanes - 1, 1), p)
 
 
-def kernel(n, L, force, modulus, out, cout, comp, fm, lam, inv, r, w, x, tmp, cg, c1, c2, clam, cinv, cf, cr, cw, ce, part, lsem, ssem, rsem, sums_s, sums_r):
+def kernel(n, L, force, modulus, out, cout, comp, fm, lam, inv, r, w, x, tmp, cg, c1, c2, clam, cinv, cf, cr, cw, ce, part, known, lsem, ssem, rsem, sums_s, sums_r):
     me = lax.axis_index("slab")
     rows, lanes = fm.shape[2], fm.shape[3]
     crows = rows // 2
     barrier = pltpu.get_barrier_semaphore()
 
-    def greet(k, carry):
-        pl.semaphore_signal(barrier, inc=1, device_id={"slab": lax.rem(me + k, n)}, device_id_type=pl.DeviceIdType.MESH)
-        return carry
-
-    lax.fori_loop(1, n, greet, 0)
+    def inside(i):
+        return jnp.logical_and(i >= 0, i < n)
+
+    def signal(sem, d):
+        @pl.when(inside(me + d))
+        def _():
+            pl.semaphore_signal(sem, inc=1, device_id={"slab": me + d}, device_id_type=pl.DeviceIdType.MESH)
+
+    greeted = 0
+    for k in range(1, REACH + 1):
+        for d in (k, -k):
+            signal(barrier, d)
+            greeted = greeted + inside(me + d).astype(jnp.int32)
+
+    def round_tell(j):
+        signal(known.at[2 * j], REACH * 2**j)
+        signal(known.at[2 * j + 1], -REACH * 2**j)
+
+    def round_hear(j):
+        pl.when(inside(me - REACH * 2**j))(lambda: pl.semaphore_wait(known.at[2 * j], 1))
+        pl.when(inside(me + REACH * 2**j))(lambda: pl.semaphore_wait(known.at[2 * j + 1], 1))
+
     own = pl.ds(H, L)
     loads = [
         pltpu.make_async_copy(force, fm.at[pl.ds(0, 3), own], lsem.at[0]),
@@ -164,9 +189,6 @@
             d, dst,
         )
 
-    def inside(i):
-        return jnp.logical_and(i >= 0, i < n)
-
     def start(name):
         cp, d, _ = copies[name]
         pl.when(inside(me + d))(cp.start)
@@ -182,19 +204,23 @@
         def _():
             dst[...] = jnp.zeros(dst.shape, jnp.float32)
 
-    def layers(name, d, lo, hi):
-        mine = fm.at[:, pl.ds(H + lo, hi - lo)]
-        theirs = fm.at[:, pl.ds(H + lo - d * L, hi - lo)]
+    def layers(name, d, part, lo, hi):
+        mine = fm.at[part, pl.ds(H + lo, hi - lo)]
+        theirs = fm.at[part, pl.ds(H + lo - d * L, hi - lo)]
         remote(name, mine, theirs, d)
 
-    layers("near+", 1, 1, L)
-    layers("near-", -1, 0, 2)
-    layers("next+", 1, 0, 1)
-    layers("next-", -1, 2, L)
-    layers("far+", 2, 0, L)
-    layers("far-", -2, 0, L - 1)
+    force3, both = pl.ds(0, 3), pl.ds(0, 4)
+    layers("near+", 1, force3, 2, L)
+    layers("near+m", 1, 3, 1, L)
+    layers("near-", -1, both, 0, 2)
+    layers("next+", 1, force3, 0, 2)
+    layers("next+m", 1, 3, 0, 1)
+    layers("next-", -1, both, 2, L)
+    layers("far+", 2, force3, 1, L)
+    layers("far+m", 2, 3, 0, L)
+    layers("far-", -2, both, 0, L - 1)
     for name, buf, reach in (("g", cg, 4), ("c1", c1, 3), ("c2", c2, 2)):
-        for k in range(1, reach + 1):
+        for k in range(2 if name == "g" else 1, reach + 1):
             for d in (k, -k):
                 remote((name, d), buf.at[reach], buf.at[reach - d], d)
 
@@ -208,17 +234,27 @@
     cscale, csteps = coefficients(*COARSE, CDEG)
     _, wsteps = coefficients(*COARSE, 2 * CDEG)
 
+    near = ("near+", "near+m", "near-")
+    rest = ("next+", "next+m", "next-")
+    far = ("far+", "far+m", "far-")
     for cp in loads:
         cp.wait()
-    pl.semaphore_wait(barrier, n - 1)
-    for name in ("near+", "near-"):
+    pl.semaphore_wait(barrier, greeted)
+    round_tell(0)
+    for name in near:
         start(name)
-    for c in range(4):
-        cg[4, c] = pack(lambda z: fm[c, H + z], tmp, 0.5 if c < 3 else 0.05, even)
-    for k in range(1, 5):
+    for name in rest:
+        start(name)
+
+    def reduced(d):
+        for c in range(4):
+            cg[4 + d, c] = pack(lambda z: fm[c, H + d * L + z], tmp, 0.5 if c < 3 else 0.05, even)
+
+    reduced(0)
+    for k in range(2, 5):
         start(("g", k))
         start(("g", -k))
-    for name in ("far+", "far-", "next+", "next-"):
+    for name in far:
         start(name)
 
     def take(lo, hi):
@@ -248,8 +284,8 @@
                 into[c, H + 2 * d] = a
                 into[c, H + 2 * d + 1] = b
 
-    wait("near+")
-    wait("near-")
+    for name in near:
+        wait(name)
     take(-3, L + 2)
     invert(lam, inv, -2, L + 2, first, last, fsh, U_FINE)
     begin(fm, inv, w, None, -2, L + 2, fscale, U_FINE)
@@ -257,7 +293,30 @@
     sweep(r, r, w, None, lam, inv, 0, L, None, None, fsh, U_FINE)
     exchange("c1", c1, 3)
 
-    for k in range(1, 5):
+    def solve(lo, hi, rhs, steps):
+        begin(rhs, cinv, cw, ce, lo, hi, cscale, U_COARSE)
+        for k, (old, new) in enumerate(steps):
+            src = rhs if k == 0 else cr
+            sweep(src, cr, cw, ce, clam, cinv, lo + k + 1, hi - k - 1, old, new, csh, U_COARSE)
+
+    def prolong(lo, hi):
+        def body(z, carry):
+            for c in range(3):
+                e = ce[c, z]
+                for half in range(2):
+                    f = 2 * (z - H) + half + H
+                    w[c, f, pl.ds(0, crows, stride=2), :] = e
+                    w[c, f, pl.ds(1, crows, stride=2), :] = e
+                    x[c, f] = x[c, f] + w[c, f]
+            return carry
+
+        loop(lo, hi, body, 0, U_COARSE)
+
+    for name in rest:
+        wait(name)
+    reduced(-1)
+    reduced(1)
+    for k in range(2, 5):
         wait(("g", k))
         wait(("g", -k))
     for d in range(-4, 5):
@@ -269,7 +328,10 @@
                 else:
                     clam[z] = v
     invert(clam, cinv, -7, 9, cfirst, clast, csh, U_COARSE)
-    for name in ("far+", "far-", "next+", "next-"):
+    gather("c1", c1, 3, cr)
+    solve(-6, 8, cr, csteps)
+
+    for name in far:
         wait(name)
     take(-8, -3)
     take(L + 2, L + 7)
@@ -279,27 +341,6 @@
     sweep(fm, r, w, x, lam, inv, -6, L + 6, fold, fnew, fsh, U_FINE)
     sweep(r, r, w, None, lam, inv, -5, L + 5, None, None, fsh, U_FINE)
 
-    def solve(lo, hi, rhs, steps):
-        begin(rhs, cinv, cw, ce, lo, hi, cscale, U_COARSE)
-        for k, (old, new) in enumerate(steps):
-            src = rhs if k == 0 else cr
-            sweep(src, cr, cw, ce, clam, cinv, lo + k + 1, hi - k - 1, old, new, csh, U_COARSE)
-
-    def prolong(lo, hi):
-        def body(z, carry):
-            for c in range(3):
-                e = ce[c, z]
-                for half in range(2):
-                    f = 2 * (z - H) + half + H
-                    w[c, f, pl.ds(0, crows, stride=2), :] = e
-                    w[c, f, pl.ds(1, crows, stride=2), :] = e
-                    x[c, f] = x[c, f] + w[c, f]
-            return carry
-
-        loop(lo, hi, body, 0, U_COARSE)
-
-    gather("c1", c1, 3, cr)
-    solve(-6, 8, cr, csteps)
     prolong(-3, 5)
     sweep(r, r, w, x, lam, inv, -5, L + 5, None, fscale, fsh, U_FINE)
     sweep(r, r, w, x, lam, inv, -4, L + 4, fold, fnew, fsh, U_FINE)
@@ -307,6 +348,10 @@
     sweep(r, r, w, x, lam, inv, -2, L + 2, fold, fnew, fsh, U_FINE)
     sweep(r, r, w, None, lam, inv, -1, L + 1, None, None, fsh, U_FINE)
     exchange("c2", c2, 2)
+
+    for j in range(1, rounds(n)):
+        round_hear(j - 1)
+        round_tell(j)
 
     solve(-7, 9, cf, wsteps)
     coarse_sum = jnp.zeros((crows, lanes), jnp.float32)
@@ -349,6 +394,7 @@
         tell(k).wait_recv()
         return carry
 
+    round_hear(rounds(n) - 1)
     lax.fori_loop(1, n, say, 0)
     for name in copies:
         cp, d, _ = copies[name]
@@ -366,25 +412,36 @@
     lax.fori_loop(1, n, done, 0)
 
 
+def hand_out(fine, coarse, comp, fine_out, coarse_out, comp_out, sem):
+    copies = [pltpu.make_async_copy(fine, fine_out, sem.at[0]), pltpu.make_async_copy(coarse, coarse_out, sem.at[1])]
+    for cp in copies:
+        cp.start()
+    for i in range(2):
+        comp_out[i] = comp[i]
+    for cp in copies:
+        cp.wait()
+
+
 def body(n, force, modulus):
     _, L, rows, lanes = force.shape
     f32 = jnp.float32
     fine, coarse = (L + 2 * H, rows, lanes), (L // 2 + 2 * H, rows // 2, lanes)
     pair = (rows // 2, lanes)
     V = pltpu.VMEM
-    remotes = 6 + 8 + 6 + 4
+    remotes = 9 + 6 + 6 + 4
     scratch = [
         V((4,) + fine, f32), V(fine, f32), V((3,) + fine, f32), V((3,) + fine, f32),
         V((3,) + fine, f32), V((3,) + fine, f32), V((2, rows, lanes), f32),
         V((9, 4) + pair, f32), V((7, 3) + pair, f32), V((5, 3) + pair, f32),
         V(coarse, f32), V((3,) + coarse, f32), V((3,) + coarse, f32), V((3,) + coarse, f32),
         V((3,) + coarse, f32), V((3,) + coarse, f32), V((n, 2, lanes), f32),
+        pltpu.SemaphoreType.REGULAR((2 * rounds(n),)),
         pltpu.SemaphoreType.DMA((2,)),
         pltpu.SemaphoreType.DMA((remotes,)), pltpu.SemaphoreType.DMA((remotes,)),
         pltpu.SemaphoreType.DMA((n,)), pltpu.SemaphoreType.DMA((n,)),
     ]
     vmem = pl.BlockSpec(memory_space=pltpu.VMEM)
-    return pl.pallas_call(
+    results = pl.pallas_call(
         functools.partial(kernel, n, L),
         out_shape=(
             jax.ShapeDtypeStruct(force.shape, f32),
@@ -396,6 +453,14 @@
         scratch_shapes=scratch,
         compiler_params=pltpu.CompilerParams(collective_id=0, has_side_effects=True),
     )(force, modulus)
+    smem = pl.BlockSpec(memory_space=pltpu.SMEM)
+    return pl.pallas_call(
+        hand_out,
+        out_shape=tuple(jax.ShapeDtypeStruct(v.shape, f32) for v in results),
+        in_specs=(vmem, vmem, smem),
+        out_specs=(pl.BlockSpec(memory_space=pl.ANY), pl.BlockSpec(memory_space=pl.ANY), smem),
+        scratch_shapes=[pltpu.SemaphoreType.DMA((2,))],
+    )(*results)
 
 
 def solution(mesh):

time: 71.5 us -> 47.3 us (0.66)
  Pallas kernels: 67.9 us -> 46.5 us
  local copies, waits for them, and re-layouts: 2.77 us -> 0 us
    pallas_call x1, Pallas kernels: 67.9 us -> 44.3 us  [body(): pl.pallas_call(functools.partial(kernel, n, L), out_shape=(jax.ShapeDtype...]
    unnamed x7 -> x0, local copies, waits for them, and re-layouts: 2.77 us -> none
    pallas_call x0 -> x1, Pallas kernels: none -> 2.16 us  [body(): pl.pallas_call(hand_out, out_shape=tuple((jax.ShapeDtypeStruct(v.shape, f...]
where the time goes in v2:
time: 47.3 us; the launch traced here: 47.1 us
  Pallas kernels  46.5 us (98%)
  between operations  0.64 us (1%)
    pallas_call x1, Pallas kernels, body(): pl.pallas_call(functools.partial(kernel, n, L), out_shape=(jax.ShapeDtype...  44.3 us
    pallas_call x1, Pallas kernels, body(): pl.pallas_call(hand_out, out_shape=tuple((jax.ShapeDtypeStruct(v.shape, f...  2.16 us

profile of v2, /device:TPU:0, one launch (start us, length us, event | category | flops | bytes accessed | tf_op | source)
XLA Modules:
  0.0 47.1 jit_solution(15705608673928967696)
XLA Ops:
  0.6 44.3 %shard_map.49 = (f32[3,4,32,128]{3,2,1,0:T(8,128)}, f32[3,2,16,64]{3,2,1,0:T(8,128)}, f32[2]{0:T(128)}) custom-call(f32[3,4,32,128]{3,2,1,0:T(8,128)} %force.1, f32[4,32,128]{2,1,0:T(8,128)} %modulus.1), custom_call_target="tpu_custom_call" | custom-call | tf_op jit(solution)/shard_map/pallas_call | solution.py:444
  45.0 2.2 %shard_map.50 = (f32[3,4,32,128]{3,2,1,0:T(8,128)}, f32[3,2,16,64]{3,2,1,0:T(8,128)}, f32[2]{0:T(128)}) custom-call(f32[3,4,32,128]{3,2,1,0:T(8,128)} %get-tuple-element.6.fine, f32[3,2,16,64]{3,2,1,0:T(8,128)} %get-tuple-element.7.coarse, f32[2]{0:T(128)} %get-tuple-element.8.comp), custom_call_target="tpu_custom_call" | custom-call | tf_op jit(solution)/shard_map/pallas_call | solution.py:457

commit v3 on v2

--- a/solution.py
+++ b/solution.py
@@ -73,8 +73,14 @@
     loop(lo, hi, body, lam[lo - 1 + H], unroll)
 
 
-def begin(src, inv, w, x, lo, hi, scale, unroll):
-    def body(z, carry):
+def parts_of(lo, hi, x, keep):
+    if x is None or keep is None:
+        return [(lo, hi, x)]
+    return [(lo, keep[0], None), (keep[0], keep[1], x), (keep[1], hi, None)]
+
+
+def begin(src, inv, w, x, lo, hi, scale, unroll, keep=None):
+    def body(x, z, carry):
         for c in range(3):
             v = inv[c, z] * src[c, z] * scale
             w[c, z] = v
@@ -82,10 +88,11 @@
                 x[c, z] = v
         return carry
 
-    loop(lo, hi, body, 0, unroll)
-
-
-def sweep(src, r, w, x, lam, inv, lo, hi, old, new, sh, unroll):
+    for a, b, kept in parts_of(lo, hi, x, keep):
+        loop(a, b, functools.partial(body, kept), 0, unroll)
+
+
+def sweep(src, r, w, x, lam, inv, lo, hi, old, new, sh, unroll, keep=None):
     ahead_x, back_x, ahead_y, back_y = sh
 
     def upward(z, u, div):
@@ -97,7 +104,7 @@
     def spread(u):
         return (ahead_x(u[0]) - u[0]) + (ahead_y(u[1]) - u[1])
 
-    def body(z, below):
+    def body(x, z, below):
         u = [w[c, z] for c in range(3)]
         gx = [ahead_x(v) - v for v in u]
         gy = [ahead_y(v) - v for v in u]
@@ -122,7 +129,10 @@
     z0 = lo - 1 + H
     u0 = [w[c, z0] for c in range(3)]
     up0, _, _ = upward(z0, u0, spread(u0))
-    loop(lo, hi, body, tuple(up0), unroll)
+    carry = tuple(up0)
+    for a, b, kept in parts_of(lo, hi, x, keep):
+        if a < b:
+            carry = loop(a, b, functools.partial(body, kept), carry, unroll)
 
 
 def pack(load, tmp, scale, even):
@@ -141,7 +151,7 @@
     return jnp.where(even, p, pltpu.roll(p, 1, 1)), jnp.where(even, pltpu.roll(p, lanes - 1, 1), p)
 
 
-def kernel(n, L, force, modulus, out, cout, comp, fm, lam, inv, r, w, x, tmp, cg, c1, c2, clam, cinv, cf, cr, cw, ce, part, known, lsem, ssem, rsem, sums_s, sums_r):
+def kernel(n, L, force, modulus, out, cout, comp, fm, lam, inv, r, w, x, tmp, cg, c1, c2, clam, cinv, cf, cr, cw, ce, part, known, cpart, lsem, ssem, rsem, sums_s, sums_r):
     me = lax.axis_index("slab")
     rows, lanes = fm.shape[2], fm.shape[3]
     crows = rows // 2
@@ -219,8 +229,12 @@
     layers("far+", 2, force3, 1, L)
     layers("far+m", 2, 3, 0, L)
     layers("far-", -2, both, 0, L - 1)
-    for name, buf, reach in (("g", cg, 4), ("c1", c1, 3), ("c2", c2, 2)):
-        for k in range(2 if name == "g" else 1, reach + 1):
+    for k in range(2, REACH + 1):
+        for d in (k, -k):
+            remote(("m", d), cg.at[4, 3], cg.at[4 - d, 3], d)
+            remote(("g", d), cg.at[4, pl.ds(0, 3)], cg.at[4 - d, pl.ds(0, 3)], d)
+    for name, buf, reach in (("c1", c1, 3), ("c2", c2, 2)):
+        for k in range(1, reach + 1):
             for d in (k, -k):
                 remote((name, d), buf.at[reach], buf.at[reach - d], d)
 
@@ -246,14 +260,14 @@
     for name in rest:
         start(name)
 
-    def reduced(d):
-        for c in range(4):
+    def reduced(d, parts):
+        for c in parts:
             cg[4 + d, c] = pack(lambda z: fm[c, H + d * L + z], tmp, 0.5 if c < 3 else 0.05, even)
 
-    reduced(0)
-    for k in range(2, 5):
-        start(("g", k))
-        start(("g", -k))
+    reduced(0, range(4))
+    for k in range(2, REACH + 1):
+        start(("m", k))
+        start(("m", -k))
     for name in far:
         start(name)
 
@@ -292,6 +306,9 @@
     sweep(fm, r, w, None, lam, inv, -1, L + 1, fold, fnew, fsh, U_FINE)
     sweep(r, r, w, None, lam, inv, 0, L, None, None, fsh, U_FINE)
     exchange("c1", c1, 3)
+    for k in range(2, REACH + 1):
+        start(("g", k))
+        start(("g", -k))
 
     def solve(lo, hi, rhs, steps):
         begin(rhs, cinv, cw, ce, lo, hi, cscale, U_COARSE)
@@ -300,33 +317,38 @@
             sweep(src, cr, cw, ce, clam, cinv, lo + k + 1, hi - k - 1, old, new, csh, U_COARSE)
 
     def prolong(lo, hi):
-        def body(z, carry):
+        def body(x, z, carry):
             for c in range(3):
                 e = ce[c, z]
                 for half in range(2):
                     f = 2 * (z - H) + half + H
                     w[c, f, pl.ds(0, crows, stride=2), :] = e
                     w[c, f, pl.ds(1, crows, stride=2), :] = e
-                    x[c, f] = x[c, f] + w[c, f]
+                    if x is not None:
+                        x[c, f] = x[c, f] + w[c, f]
             return carry
 
-        loop(lo, hi, body, 0, U_COARSE)
+        for a, b, kept in parts_of(lo, hi, x, (0, L // 2)):
+            loop(a, b, functools.partial(body, kept), 0, U_COARSE)
 
     for name in rest:
         wait(name)
-    reduced(-1)
-    reduced(1)
-    for k in range(2, 5):
-        wait(("g", k))
-        wait(("g", -k))
-    for d in range(-4, 5):
-        for c in range(4):
-            a, b = unpack(cg[4 + d, c], even)
-            for z, v in ((H + 2 * d, a), (H + 2 * d + 1, b)):
-                if c < 3:
-                    cf[c, z] = v
-                else:
-                    clam[z] = v
+    def spread_out(parts):
+        for d in range(-REACH, REACH + 1):
+            for c in parts:
+                a, b = unpack(cg[4 + d, c], even)
+                for z, v in ((H + 2 * d, a), (H + 2 * d + 1, b)):
+                    if c < 3:
+                        cf[c, z] = v
+                    else:
+                        clam[z] = v
+
+    reduced(-1, (3,))
+    reduced(1, (3,))
+    for k in range(2, REACH + 1):
+        wait(("m", k))
+        wait(("m", -k))
+    spread_out((3,))
     invert(clam, cinv, -7, 9, cfirst, clast, csh, U_COARSE)
     gather("c1", c1, 3, cr)
     solve(-6, 8, cr, csteps)
@@ -337,15 +359,15 @@
     take(L + 2, L + 7)
     invert(lam, inv, -7, -2, first, last, fsh, U_FINE)
     invert(lam, inv, L + 2, L + 7, first, last, fsh, U_FINE)
-    begin(fm, inv, w, x, -7, L + 7, fscale, U_FINE)
-    sweep(fm, r, w, x, lam, inv, -6, L + 6, fold, fnew, fsh, U_FINE)
+    begin(fm, inv, w, x, -7, L + 7, fscale, U_FINE, (0, L))
+    sweep(fm, r, w, x, lam, inv, -6, L + 6, fold, fnew, fsh, U_FINE, (0, L))
     sweep(r, r, w, None, lam, inv, -5, L + 5, None, None, fsh, U_FINE)
 
     prolong(-3, 5)
-    sweep(r, r, w, x, lam, inv, -5, L + 5, None, fscale, fsh, U_FINE)
-    sweep(r, r, w, x, lam, inv, -4, L + 4, fold, fnew, fsh, U_FINE)
-    sweep(r, r, w, x, lam, inv, -3, L + 3, None, fscale, fsh, U_FINE)
-    sweep(r, r, w, x, lam, inv, -2, L + 2, fold, fnew, fsh, U_FINE)
+    sweep(r, r, w, x, lam, inv, -5, L + 5, None, fscale, fsh, U_FINE, (0, L))
+    sweep(r, r, w, x, lam, inv, -4, L + 4, fold, fnew, fsh, U_FINE, (0, L))
+    sweep(r, r, w, x, lam, inv, -3, L + 3, None, fscale, fsh, U_FINE, (0, L))
+    sweep(r, r, w, x, lam, inv, -2, L + 2, fold, fnew, fsh, U_FINE, (0, L))
     sweep(r, r, w, None, lam, inv, -1, L + 1, None, None, fsh, U_FINE)
     exchange("c2", c2, 2)
 
@@ -353,6 +375,12 @@
         round_hear(j - 1)
         round_tell(j)
 
+    reduced(-1, range(3))
+    reduced(1, range(3))
+    for k in range(2, REACH + 1):
+        wait(("g", k))
+        wait(("g", -k))
+    spread_out(range(3))
     solve(-7, 9, cf, wsteps)
     coarse_sum = jnp.zeros((crows, lanes), jnp.float32)
     pick = (
@@ -363,22 +391,25 @@
         for z in range(L // 2):
             v = ce[c, H + z]
             coarse_sum = coarse_sum + v * cf[c, H + z]
-            cout[c, z] = jnp.dot(v, pick, precision=lax.Precision.HIGHEST, preferred_element_type=jnp.float32)
+            cpart[c, z] = jnp.dot(v, pick, precision=lax.Precision.HIGHEST, preferred_element_type=jnp.float32)
+
+    coarse_out = pltpu.make_async_copy(cpart, cout, lsem.at[2])
+    coarse_out.start()
 
     gather("c2", c2, 2, cr)
     solve(-4, 6, cr, csteps)
     prolong(-1, 3)
-    sweep(r, r, w, x, lam, inv, -1, L + 1, None, fscale, fsh, U_FINE)
-    sweep(r, r, w, x, lam, inv, 0, L, fold, fnew, fsh, U_FINE)
+    sweep(r, r, w, x, lam, inv, -1, L + 1, None, fscale, fsh, U_FINE, (0, L))
+    sweep(r, r, w, x, lam, inv, 0, L, fold, fnew, fsh, U_FINE, (0, L))
 
     fine_sum = jnp.zeros((rows, lanes), jnp.float32)
     for c in range(3):
         for z in range(L):
-            v = x[c, H + z]
-            out[c, z] = v
-            fine_sum = fine_sum + v * fm[c, H + z]
+            fine_sum = fine_sum + x[c, H + z] * fm[c, H + z]
     part[0, 0:1] = jnp.sum(fine_sum, axis=0, keepdims=True)
     part[0, 1:2] = jnp.sum(coarse_sum, axis=0, keepdims=True)
+
+    fine_out = pltpu.make_async_copy(x.at[:, own], out, lsem.at[3])
 
     def tell(k):
         return pltpu.make_async_remote_copy(
@@ -396,6 +427,7 @@
 
     round_hear(rounds(n) - 1)
     lax.fori_loop(1, n, say, 0)
+    fine_out.start()
     for name in copies:
         cp, d, _ = copies[name]
         pl.when(inside(me + d))(cp.wait_send)
@@ -410,6 +442,8 @@
         return carry
 
     lax.fori_loop(1, n, done, 0)
+    coarse_out.wait()
+    fine_out.wait()
 
 
 def hand_out(fine, coarse, comp, fine_out, coarse_out, comp_out, sem):
@@ -428,7 +462,7 @@
     fine, coarse = (L + 2 * H, rows, lanes), (L // 2 + 2 * H, rows // 2, lanes)
     pair = (rows // 2, lanes)
     V = pltpu.VMEM
-    remotes = 9 + 6 + 6 + 4
+    remotes = 9 + 6 + 6 + 6 + 4
     scratch = [
         V((4,) + fine, f32), V(fine, f32), V((3,) + fine, f32), V((3,) + fine, f32),
         V((3,) + fine, f32), V((3,) + fine, f32), V((2, rows, lanes), f32),
@@ -436,7 +470,8 @@
         V(coarse, f32), V((3,) + coarse, f32), V((3,) + coarse, f32), V((3,) + coarse, f32),
         V((3,) + coarse, f32), V((3,) + coarse, f32), V((n, 2, lanes), f32),
         pltpu.SemaphoreType.REGULAR((2 * rounds(n),)),
-        pltpu.SemaphoreType.DMA((2,)),
+        V((3, L // 2, rows // 2, lanes // 2), f32),
+        pltpu.SemaphoreType.DMA((4,)),
         pltpu.SemaphoreType.DMA((remotes,)), pltpu.SemaphoreType.DMA((remotes,)),
         pltpu.SemaphoreType.DMA((n,)), pltpu.SemaphoreType.DMA((n,)),
     ]
@@ -449,7 +484,7 @@
             jax.ShapeDtypeStruct((2,), f32),
         ),
         in_specs=[pl.BlockSpec(memory_space=pl.ANY)] * 2,
-        out_specs=(vmem, vmem, pl.BlockSpec(memory_space=pltpu.SMEM)),
+        out_specs=(pl.BlockSpec(memory_space=pl.ANY), pl.BlockSpec(memory_space=pl.ANY), pl.BlockSpec(memory_space=pltpu.SMEM)),
         scratch_shapes=scratch,
         compiler_params=pltpu.CompilerParams(collective_id=0, has_side_effects=True),
     )(force, modulus)

time: 47.3 us -> 46.8 us (0.989)
  Pallas kernels: 46.5 us -> 46 us
    pallas_call x1, Pallas kernels: 44.3 us -> 43.8 us  [body(): pl.pallas_call(functools.partial(kernel, n, L), out_shape=(jax.ShapeDtype...]
where the time goes in v3:
time: 46.8 us; the launch traced here: 46.6 us
  Pallas kernels  46 us (98%)
  between operations  0.64 us (1%)
    pallas_call x1, Pallas kernels, body(): pl.pallas_call(functools.partial(kernel, n, L), out_shape=(jax.ShapeDtype...  43.8 us
    pallas_call x1, Pallas kernels, body(): pl.pallas_call(hand_out, out_shape=tuple((jax.ShapeDtypeStruct(v.shape, f...  2.16 us

profile of v3, /device:TPU:0, one launch (start us, length us, event | category | flops | bytes accessed | tf_op | source)
XLA Modules:
  0.0 46.6 jit_solution(11828487695581137441)
XLA Ops:
  0.6 43.8 %shard_map.49 = (f32[3,4,32,128]{3,2,1,0:T(8,128)}, f32[3,2,16,64]{3,2,1,0:T(8,128)}, f32[2]{0:T(128)}) custom-call(f32[3,4,32,128]{3,2,1,0:T(8,128)} %force.1, f32[4,32,128]{2,1,0:T(8,128)} %modulus.1), custom_call_target="tpu_custom_call" | custom-call | tf_op jit(solution)/shard_map/pallas_call | solution.py:479
  44.5 2.2 %shard_map.50 = (f32[3,4,32,128]{3,2,1,0:T(8,128)}, f32[3,2,16,64]{3,2,1,0:T(8,128)}, f32[2]{0:T(128)}) custom-call(f32[3,4,32,128]{3,2,1,0:T(8,128)} %get-tuple-element.6.fine, f32[3,2,16,64]{3,2,1,0:T(8,128)} %get-tuple-element.7.coarse, f32[2]{0:T(128)} %get-tuple-element.8.comp), custom_call_target="tpu_custom_call" | custom-call | tf_op jit(solution)/shard_map/pallas_call | solution.py:492
